TPU v7x, 32 devices: a whole 2x2x4 slice. The times are simulated.
32 devices in a mesh: groups: 1, row: 32 (over z, y, x, core).
Axes of the slice: x: 2, y: 2, z: 4, core: 2. Of those that a mesh axis runs over, the one named last changes fastest.
Arguments:
- pair_mantissa: bfloat16 [128, 128, 128], P(('groups', 'row')), may hold values from -6 to 6
- pair_exponent: int32 [128, 1, 128], P(('groups', 'row')), may hold values from -3 to 3
- residue_mask: int32 [128], P('groups'), may hold values 0 or 1
- ln_gain: float32 [128], replicated, may hold values from 0.25 to 1.75
- ln_shift: float32 [128], replicated, may hold values from -3 to 3
- w_proj: bfloat16 [128, 512], replicated, may hold values from -10 to 10
- w_bias: bfloat16 [128, 4], replicated, may hold values from -0.5 to 0.5
- gate_shift: float32 [128], replicated, may hold values from -4 to 4
- w_out: bfloat16 [128, 128], replicated, may hold values from -0.5 to 0.5
- out_shift: float32 [128], replicated, may hold values from -3 to 3
Outputs:
- update: bfloat16 [32, 128, 128], P(('groups', 'row'))
All inputs are finite; a program needn't handle non-finite values.
Results may differ from a plain program's by a relative error of at most 0.005.
Values may be sent and summed in bfloat16 or wider, within the bound.
A program may use at most 64 MiB of HBM per device.

v0:
```python
import jax
import jax.numpy as jnp
from jax import lax
from jax.sharding import PartitionSpec as P

WD = 1
epsilon = 1e-05
big_negative = 1000000000.0


def dequantize(mantissa, exponent):
    scaling = jnp.zeros(exponent.shape, jnp.float32)
    for expo_level in range(-3, 4):
        scaling = scaling + jnp.where(
            exponent == expo_level, jnp.float32(2.0**expo_level), jnp.float32(0.0)
        )
    row_count, block_count, channels = exponent.shape
    block_width = mantissa.shape[1] // block_count
    scaling = jnp.broadcast_to(
        scaling[:, :, None, :], (row_count, block_count, block_width, channels)
    )
    return mantissa.astype(jnp.float32) * scaling.reshape(
        row_count, block_count * block_width, channels
    )


def normalize(mantissa, exponent, ln_gain, ln_shift):
    values = dequantize(mantissa, exponent)
    center = jnp.mean(values, axis=-1, keepdims=True)
    spread = jnp.mean(jnp.square(values - center), axis=-1, keepdims=True)
    return ((values - center) * lax.rsqrt(spread + epsilon) * ln_gain + ln_shift).astype(
        jnp.bfloat16
    )


def project(columns, w_proj, gate_shift, inner_width, window_rows, head_size):
    key_value = jnp.einsum(
        "lmc,cd->mld",
        columns,
        w_proj[:, inner_width : 3 * inner_width],
        preferred_element_type=jnp.float32,
    ).astype(jnp.bfloat16)
    query_weight = jnp.concatenate([w_proj[:, :inner_width], w_proj[:, 3 * inner_width :]], axis=1)
    query_gate = jnp.einsum(
        "wmc,cd->mwd", columns[:window_rows], query_weight, preferred_element_type=jnp.float32
    )
    queries = (query_gate[..., :inner_width] * head_size ** (-0.5)).astype(jnp.bfloat16)
    gating = jax.nn.sigmoid(query_gate[..., inner_width:] + gate_shift)
    return (key_value, queries, gating)


def finish(gating, attended, w_out, out_shift):
    gated_out = (gating * attended).astype(jnp.bfloat16)
    return (
        jnp.einsum("mwd,dc->mwc", gated_out, w_out, preferred_element_type=jnp.float32) + out_shift
    ).astype(jnp.bfloat16)


def attend_whole(columns, key_bias, mask_bias, w_proj, gate_shift, w_out, out_shift):
    inner_width = w_out.shape[0]
    head_count = key_bias.shape[1]
    head_size = inner_width // head_count
    window_rows = key_bias.shape[2]
    key_value, queries, gating = project(
        columns, w_proj, gate_shift, inner_width, window_rows, head_size
    )

    def single_column(operands):
        kv_column, query_column = operands
        key_heads = kv_column[:, :inner_width].reshape(-1, head_count, head_size)
        value_heads = kv_column[:, inner_width:].reshape(-1, head_count, head_size)
        query_heads = query_column.reshape(window_rows, head_count, head_size)
        scores = jnp.einsum(
            "lhd,whd->lhw", key_heads, query_heads, preferred_element_type=jnp.float32
        )
        scores = scores + key_bias.astype(jnp.float32) + mask_bias[:, None, None]
        row_max = jnp.max(scores, axis=0)
        weights = jnp.exp(scores - row_max)
        denominator = jnp.sum(weights, axis=0)
        attended = jnp.einsum(
            "lhw,lhd->whd",
            weights.astype(jnp.bfloat16),
            value_heads,
            preferred_element_type=jnp.float32,
        )
        return (attended / denominator.T[:, :, None]).reshape(window_rows, inner_width)

    attended = lax.map(single_column, (key_value, queries))
    return finish(gating, attended, w_out, out_shift)


def per_device(
    pair_mantissa,
    pair_exponent,
    residue_mask,
    ln_gain,
    ln_shift,
    w_proj,
    w_bias,
    gate_shift,
    w_out,
    out_shift,
):
    devices_row = lax.axis_size("row")
    local_rows = pair_mantissa.shape[0]
    channels = pair_mantissa.shape[2]
    window_rows = WD * devices_row
    normal = normalize(pair_mantissa, pair_exponent, ln_gain, ln_shift)
    local_bias = jnp.einsum(
        "rwc,ch->rhw", normal[:, :window_rows], w_bias, preferred_element_type=jnp.float32
    ).astype(jnp.bfloat16)
    mask_bias = big_negative * (residue_mask.astype(jnp.float32) - 1.0)
    split_pair = normal.reshape(local_rows, devices_row, local_rows, channels)
    key_bias = lax.all_gather(local_bias, "row", axis=0, tiled=True)
    received = lax.all_to_all(split_pair, "row", split_axis=1, concat_axis=0, tiled=True)
    result = attend_whole(received[:, 0], key_bias, mask_bias, w_proj, gate_shift, w_out, out_shift)
    row_layout = lax.all_to_all(result, "row", split_axis=1, concat_axis=0, tiled=True)
    return jnp.transpose(row_layout, (1, 0, 2))


def solution(mesh):
    in_specs = (
        P(("groups", "row"), None, None),
        P(("groups", "row"), None, None),
        P("groups"),
        P(),
        P(),
        P(),
        P(),
        P(),
        P(),
        P(),
    )
    out_specs = P(("groups", "row"), None, None)
    return jax.shard_map(
        per_device, mesh=mesh, in_specs=in_specs, out_specs=out_specs, check_vma=False
    )
```

profile of v0, /device:TPU:0, one launch (start us, length us, event | category | flops | bytes accessed | tf_op | source)
XLA Modules:
  0.0 68.8 jit_solution(6774469167850363746)
XLA Ops:
  0.0 0.7 %fusion.32 = f32[4,1,128]{2,1,0:T(1,128)S(1)} fusion(s32[4,1,128]{2,1,0:T(1,128)} %param.13), kind=kLoop, calls=%fused_computation.53 | loop fusion | flops 10240 | bytes 4096 | tf_op jit(solution)/shard_map/add | solution.py:14
  0.7 1.1 %fusion.12 = f32[4,128]{1,0:T(4,128)S(1)} fusion(bf16[4,128,128]{2,1,0:T(8,128)(2,1)} %param.12, f32[4,128]{1,0:T(4,128)S(1)} %bitcast.76), kind=kLoop, calls=%fused_computation.24 | loop fusion | flops 196096 | bytes 135168 | tf_op jit(solution)/shard_map/reduce_sum | solution.py:29
  1.8 0.2 multiply_reduce_fusion
  2.1 0.0 copy-start.3
  2.1 0.0 copy-start.4
  2.1 0.6 copy-done.3
  2.7 0.0 copy-done.4
  2.7 0.2 add_convert_fusion
  2.9 0.7 %copy.18 = bf16[4,32,4,128]{3,0,2,1:T(4,128)(2,1)} copy(bf16[4,32,4,128]{3,2,1,0:T(4,128)(2,1)S(1)} %bitcast.72) | data formatting | bytes 262144 | tf_op jit(solution)/shard_map/reshape | solution.py:113
  3.7 7.3 %all-to-all-start = ((bf16[4,32,4,128]{3,0,2,1:T(4,128)(2,1)}), bf16[4,32,4,128]{3,0,2,1:T(4,128)(2,1)S(1)}, u32[]{:S(2)}, u32[]{:S(2)}) async-start(bf16[4,32,4,128]{3,0,2,1:T(4,128)(2,1)} %copy.18), calls=%async_computation | async-start | bytes 262144 | tf_op jit(solution)/shard_map/all_to_all | solution.py:115
  11.0 0.0 copy-start.6
  11.1 0.1 fusion.10
  11.2 0.5 copy-done.6
  11.7 42.2 %all_gather.3 = bf16[128,4,32]{2,1,0:T(4,128)(2,1)S(1)} all-gather(bf16[4,4,32]{2,1,0:T(4,128)(2,1)S(1)} %fusion.10), channel_id=1, replica_groups=mesh['groups'=1,'row'=32] {'row'}, dimensions={0}, use_global_device_ids=true | all-gather | bytes 33792 | tf_op jit(solution)/shard_map/all_gather | solution.py:114
  53.9 0.1 copy.22
  54.2 0.2 convolution_bitcast_fusion.2
  54.3 0.2 fusion.8
  54.6 3.8 %while.10 = (s32[]{:T(128)}, f32[4,32,128]{2,1,0:T(8,128)S(1)}, bf16[4,128,256]{2,1,0:T(8,128)(2,1)S(1)}, bf16[4,32,128]{2,1,0:T(8,128)(2,1)S(1)}, bf16[128,4,32...) while((s32[]{:T(128)}, f32[4,32,128]{2,1,0:T(8,128)S(1)}, bf16[4,128,256]{2,1,0:T(8,128)(2,1)S(1)}, ...), condition=%wide.region_5.6_spmd, body=%wide.region_2.5_spmd.sunk | while | flops 2232066 | bytes 814169 | solution.py:88
  54.6 0.1 copy.38
  54.7 0.1 reshape.53
  54.8 0.2 fusion.54
  55.0 0.2 fusion.55
  55.2 0.2 fusion.56
  55.4 0.1 copy.39
  55.5 0.1 copy.38
  55.7 0.1 reshape.53
  55.8 0.2 fusion.54
  56.0 0.2 fusion.55
  56.2 0.2 fusion.56
  56.4 0.1 copy.39
  56.5 0.1 copy.38
  56.6 0.1 reshape.53
  56.7 0.2 fusion.54
  56.9 0.2 fusion.55
  57.1 0.2 fusion.56
  57.3 0.1 copy.39
  57.4 0.1 copy.38
  57.6 0.1 reshape.53
  57.7 0.2 fusion.54
  57.9 0.2 fusion.55
  58.1 0.2 fusion.56
  58.3 0.1 copy.39
  58.3 0.0 copy-start.7
  58.4 0.6 copy-done.7
  59.0 0.0 copy-done.8
  59.0 0.1 fusion.9
  59.2 9.0 %all_to_all.30 = bf16[4,32,128]{2,0,1:T(4,128)(2,1)S(1)} all-to-all(bf16[4,32,128]{2,0,1:T(4,128)(2,1)S(1)} %copy.24), channel_id=1, replica_groups=mesh['groups'=1,'row'=32] {'row'}, dimensions={1} | all-to-all | bytes 65536 | tf_op jit(solution)/shard_map/all_to_all | solution.py:117
  68.2 0.6 copy.50
  (36 shorter events, 0.3 us)
Async XLA Ops:
  0.0 58.4 %copy-start = (bf16[128,128]{1,0:T(8,128)(2,1)S(1)}, bf16[128,128]{1,0:T(8,128)(2,1)}, u32[]{:S(2)}) copy-start(bf16[128,128]{1,0:T(8,128)(2,1)} %param.20) | copy-start | bytes 98308
  0.0 1.8 %copy-start.1 = (bf16[4,128,128]{2,1,0:T(8,128)(2,1)S(1)}, bf16[4,128,128]{2,1,0:T(8,128)(2,1)}, u32[]{:S(2)}) copy-start(bf16[4,128,128]{2,1,0:T(8,128)(2,1)} %param.12) | copy-start | bytes 393220
  2.1 0.7 copy-start.3
  2.1 0.7 copy-start.4
  3.7 7.3 %copy-start.5 = (bf16[128,4]{0,1:T(4,128)(2,1)S(1)}, bf16[128,4]{0,1:T(4,128)(2,1)}, u32[]{:S(2)}) copy-start(bf16[128,4]{0,1:T(4,128)(2,1)} %param.18) | copy-start | bytes 3076
  3.7 50.4 %all-to-all-start = ((bf16[4,32,4,128]{3,0,2,1:T(4,128)(2,1)}), bf16[4,32,4,128]{3,0,2,1:T(4,128)(2,1)S(1)}, u32[]{:S(2)}, u32[]{:S(2)}) async-start(bf16[4,32,4,128]{3,0,2,1:T(4,128)(2,1)} %copy.18), calls=%async_computation | async-start | bytes 262144 | tf_op jit(solution)/shard_map/all_to_all | solution.py:115
  11.0 0.7 copy-start.6
  11.7 42.3 %copy-start.2 = (bf16[128,512]{1,0:T(8,128)(2,1)S(1)}, bf16[128,512]{1,0:T(8,128)(2,1)}, u32[]{:S(2)}) copy-start(bf16[128,512]{1,0:T(8,128)(2,1)} %param.17) | copy-start | bytes 393220
  58.3 0.7 copy-start.7
  58.4 0.7 copy-start.8
where the time goes:
time: 69 us; the launch traced here: 68.8 us
  blocking collectives  51.2 us (74%)
  starting transfers between devices  7.33 us (11%)
  local copies, waits for them, and re-layouts  4.59 us (7%)
  other arithmetic  2.97 us (4%)
  matrix products  2.33 us (3%)
    all_gather x1, blocking collectives, per_device(): key_bias = lax.all_gather(local_bias, 'row', axis=0, tiled=True)  42.2 us
    all_to_all x1, blocking collectives, per_device(): lax.all_to_all(result, 'row', split_axis=1, concat_axis=0, tiled=True)  8.95 us
    all_to_all x1, starting transfers between devices, per_device(): lax.all_to_all(split_pair, 'row', split_axis=1, concat_axis=0, tiled=True)  7.33 us
    unnamed x19, local copies, waits for them, and re-layouts  2.47 us
  transfers between devices with their start and end apart: 1, of which 0 were waited for; matrix products, arithmetic and copies ran while one was open for 0% of the time, Pallas kernels for 0%

commit v1 on v0

--- a/solution.py
+++ b/solution.py
@@ -112,7 +112,10 @@
     mask_bias = big_negative * (residue_mask.astype(jnp.float32) - 1.0)
     split_pair = normal.reshape(local_rows, devices_row, local_rows, channels)
     key_bias = lax.all_gather(local_bias, "row", axis=0, tiled=True)
-    received = lax.all_to_all(split_pair, "row", split_axis=1, concat_axis=0, tiled=True)
+    received = jnp.concatenate(
+        lax.all_to_all(jnp.stack(jnp.split(split_pair, lax.axis_size("row"), axis=1)), "row", 0, 0),
+        axis=0,
+    )
     result = attend_whole(received[:, 0], key_bias, mask_bias, w_proj, gate_shift, w_out, out_shift)
     row_layout = lax.all_to_all(result, "row", split_axis=1, concat_axis=0, tiled=True)
     return jnp.transpose(row_layout, (1, 0, 2))

time: 69 us -> 87.4 us (1.27)
  local copies, waits for them, and re-layouts: 4.59 us -> 22.9 us
    unnamed x19 -> x50, local copies, waits for them, and re-layouts: 2.47 us -> 20.9 us
where the time goes in v1:
time: 87.4 us; the launch traced here: 87.1 us
  blocking collectives  51.2 us (59%)
  local copies, waits for them, and re-layouts  22.9 us (26%)
  starting transfers between devices  7.33 us (8%)
  other arithmetic  2.97 us (3%)
  matrix products  2.33 us (3%)
    all_gather x1, blocking collectives, per_device(): key_bias = lax.all_gather(local_bias, 'row', axis=0, tiled=True)  42.2 us
    unnamed x50, local copies, waits for them, and re-layouts  20.9 us
    all_to_all x1, blocking collectives, per_device(): lax.all_to_all(result, 'row', split_axis=1, concat_axis=0, tiled=True)  8.95 us
    all_to_all x1, starting transfers between devices, per_device(): lax.all_to_all(jnp.stack(jnp.split(split_pair, lax.axis_size('row'), axis...  7.33 us
  transfers between devices with their start and end apart: 1, of which 0 were waited for; matrix products, arithmetic and copies ran while one was open for 0% of the time, Pallas kernels for 0%

profile of v1, /device:TPU:0, one launch (start us, length us, event | category | flops | bytes accessed | tf_op | source)
XLA Modules:
  0.0 87.1 jit_solution(5746787307515938993)
XLA Ops:
  0.0 0.7 fusion.32
  0.7 1.1 %fusion.12 = f32[4,128]{1,0:T(4,128)S(1)} fusion(bf16[4,128,128]{2,1,0:T(8,128)(2,1)} %param.12, f32[4,128]{1,0:T(4,128)S(1)} %bitcast.200), kind=kLoop, calls=%fused_computation.24 | loop fusion | flops 196096 | bytes 135168 | tf_op jit(solution)/shard_map/reduce_sum | solution.py:29
  1.8 0.2 multiply_reduce_fusion
  2.1 0.6 copy-done.3
  3.0 0.6 constant_dynamic-update-slice_fusion.32
  3.6 0.6 constant_dynamic-update-slice_fusion.31
  4.2 0.6 constant_dynamic-update-slice_fusion.30
  4.8 0.6 constant_dynamic-update-slice_fusion.29
  5.4 0.6 constant_dynamic-update-slice_fusion.28
  6.0 0.6 constant_dynamic-update-slice_fusion.27
  6.6 0.6 constant_dynamic-update-slice_fusion.26
  7.2 0.6 constant_dynamic-update-slice_fusion.25
  7.8 0.6 constant_dynamic-update-slice_fusion.24
  8.4 0.6 constant_dynamic-update-slice_fusion.23
  9.0 0.6 constant_dynamic-update-slice_fusion.22
  9.6 0.6 constant_dynamic-update-slice_fusion.21
  10.1 0.6 constant_dynamic-update-slice_fusion.20
  10.7 0.6 constant_dynamic-update-slice_fusion.19
  11.3 0.6 constant_dynamic-update-slice_fusion.18
  11.9 0.6 constant_dynamic-update-slice_fusion.17
  12.5 0.6 constant_dynamic-update-slice_fusion.16
  13.1 0.6 constant_dynamic-update-slice_fusion.15
  13.7 0.6 constant_dynamic-update-slice_fusion.14
  14.3 0.6 constant_dynamic-update-slice_fusion.13
  14.9 0.6 constant_dynamic-update-slice_fusion.12
  15.5 0.6 constant_dynamic-update-slice_fusion.11
  16.1 0.6 constant_dynamic-update-slice_fusion.10
  16.7 0.6 constant_dynamic-update-slice_fusion.9
  17.3 0.6 constant_dynamic-update-slice_fusion.8
  17.9 0.6 constant_dynamic-update-slice_fusion.7
  18.5 0.6 constant_dynamic-update-slice_fusion.6
  19.1 0.6 constant_dynamic-update-slice_fusion.5
  19.7 0.6 constant_dynamic-update-slice_fusion.4
  20.2 0.6 constant_dynamic-update-slice_fusion.3
  20.8 0.6 constant_dynamic-update-slice_fusion.2
  21.4 0.6 constant_dynamic-update-slice_fusion.1
  22.0 7.3 %all-to-all-start = ((bf16[32,4,1,4,128]{4,1,3,2,0:T(4,128)(2,1)}), bf16[32,4,1,4,128]{4,1,3,2,0:T(4,128)(2,1)S(1)}, u32[]{:S(2)}, u32[]{:S(2)}) async-start(bf16[32,4,1,4,128]{4,1,3,2,0:T(4,128)(2,1)} %constant_dynamic-update-slice_fusion.1), calls=%async_computation | async-start | bytes 262144 | tf_op jit(solution)/shard_map/all_to_all | solution.py:116
  29.5 0.5 copy-done.6
  30.0 42.2 %all_gather.3 = bf16[128,4,32]{2,1,0:T(4,128)(2,1)S(1)} all-gather(bf16[4,4,32]{2,1,0:T(4,128)(2,1)S(1)} %fusion.10), channel_id=1, replica_groups=mesh['groups'=1,'row'=32] {'row'}, dimensions={0}, use_global_device_ids=true | all-gather | bytes 33792 | tf_op jit(solution)/shard_map/all_gather | solution.py:114
  72.9 3.8 %while.10 = (s32[]{:T(128)}, f32[4,32,128]{2,1,0:T(8,128)S(1)}, bf16[4,128,256]{2,1,0:T(8,128)(2,1)S(1)}, bf16[4,32,128]{2,1,0:T(8,128)(2,1)S(1)}, bf16[128,4,32...) while((s32[]{:T(128)}, f32[4,32,128]{2,1,0:T(8,128)S(1)}, bf16[4,128,256]{2,1,0:T(8,128)(2,1)S(1)}, ...), condition=%wide.region_5.6_spmd, body=%wide.region_2.5_spmd.sunk | while | flops 2232066 | bytes 814169 | solution.py:88
  73.1 0.2 fusion.56
  74.1 0.2 fusion.56
  74.5 0.2 fusion.58
  76.0 0.2 fusion.56
  76.4 0.2 fusion.58
  76.7 0.6 copy-done.7
  77.5 9.0 %all_to_all.20 = bf16[4,32,128]{2,0,1:T(4,128)(2,1)S(1)} all-to-all(bf16[4,32,128]{2,0,1:T(4,128)(2,1)S(1)} %copy.117), channel_id=1, replica_groups=mesh['groups'=1,'row'=32] {'row'}, dimensions={1} | all-to-all | bytes 65536 | tf_op jit(solution)/shard_map/all_to_all | solution.py:120
  86.5 0.6 copy.302
  (69 shorter events, 3.7 us)
Async XLA Ops:
  0.0 76.7 %copy-start = (bf16[128,128]{1,0:T(8,128)(2,1)S(1)}, bf16[128,128]{1,0:T(8,128)(2,1)}, u32[]{:S(2)}) copy-start(bf16[128,128]{1,0:T(8,128)(2,1)} %param.20) | copy-start | bytes 98308
  0.0 1.8 %copy-start.1 = (bf16[4,128,128]{2,1,0:T(8,128)(2,1)S(1)}, bf16[4,128,128]{2,1,0:T(8,128)(2,1)}, u32[]{:S(2)}) copy-start(bf16[4,128,128]{2,1,0:T(8,128)(2,1)} %param.12) | copy-start | bytes 393220
  2.1 0.7 copy-start.3
  2.1 0.7 copy-start.4
  22.0 7.3 %copy-start.5 = (bf16[128,4]{0,1:T(4,128)(2,1)S(1)}, bf16[128,4]{0,1:T(4,128)(2,1)}, u32[]{:S(2)}) copy-start(bf16[128,4]{0,1:T(4,128)(2,1)} %param.18) | copy-start | bytes 3076
  22.0 50.4 %all-to-all-start = ((bf16[32,4,1,4,128]{4,1,3,2,0:T(4,128)(2,1)}), bf16[32,4,1,4,128]{4,1,3,2,0:T(4,128)(2,1)S(1)}, u32[]{:S(2)}, u32[]{:S(2)}) async-start(bf16[32,4,1,4,128]{4,1,3,2,0:T(4,128)(2,1)} %constant_dynamic-update-slice_fusion.1), calls=%async_computation | async-start | bytes 262144 | tf_op jit(solution)/shard_map/all_to_all | solution.py:116
  29.4 0.7 copy-start.6
  30.0 42.3 %copy-start.2 = (bf16[128,512]{1,0:T(8,128)(2,1)S(1)}, bf16[128,512]{1,0:T(8,128)(2,1)}, u32[]{:S(2)}) copy-start(bf16[128,512]{1,0:T(8,128)(2,1)} %param.17) | copy-start | bytes 393220
  76.7 0.7 copy-start.7
  76.7 0.7 copy-start.8
